TPU v7x, 128 devices: a whole 4x4x4 slice. The times are simulated.
128 devices in a mesh: row: 32 (over z, y, core), col: 4 (over x).
Axes of the slice: x: 4, y: 4, z: 4, core: 2. Of those that a mesh axis runs over, the one named last changes fastest.
Arguments:
- tokens: bfloat16 [16384, 2048], P('row', 'col'), may hold values from -6 to 6
- cotangent: bfloat16 [16384, 2048], P('row', 'col'), may hold values from -6 to 6
- destination: int32 [16384], P('row'), may hold values from 0 to 16383, as said below
- segment_ids: int32 [16384], P('row'), may hold values from 0 to 7, as said below
- attn_gain: float32 [2048], replicated, may hold values from 0.5 to 1.5
- w_query: bfloat16 [2048, 2048], P('row', 'col'), may hold values from -0.125 to 0.125
- w_key: bfloat16 [2048, 256], P('row', 'col'), may hold values from -0.125 to 0.125
- w_value: bfloat16 [2048, 256], P('row', 'col'), may hold values from -0.125 to 0.125
- w_output: bfloat16 [2048, 2048], P('row', 'col'), may hold values from -0.5 to 0.5
- ffn_gain: float32 [2048], replicated, may hold values from 0.5 to 1.5
- w_gate: bfloat16 [2048, 5632], P('row', 'col'), may hold values from -0.125 to 0.125
- w_up: bfloat16 [2048, 5632], P('row', 'col'), may hold values from -0.125 to 0.125
- w_down: bfloat16 [2048, 5632], P('row', 'col'), may hold values from -0.078125 to 0.078125
Outputs:
- output: bfloat16 [16384, 2048], P('row', 'col')
- input_grad: bfloat16 [16384, 2048], P('row', 'col')
- attn_gain_grad: float32 [2048], P('row')
- w_query_grad: float32 [2048, 2048], P('row', 'col')
- w_key_grad: float32 [2048, 256], P('row', 'col')
- w_value_grad: float32 [2048, 256], P('row', 'col')
- w_output_grad: float32 [2048, 2048], P('row', 'col')
- ffn_gain_grad: float32 [2048], P('row')
- w_gate_grad: float32 [2048, 5632], P('row', 'col')
- w_up_grad: float32 [2048, 5632], P('row', 'col')
- w_down_grad: float32 [2048, 5632], P('row', 'col')
Inputs may be any that keep to these rules, and one draw needn't show every extreme that they name: `destination`: A permutation; the tokens of each aligned block of 512 arriving tokens go to exactly 16 places in each aligned block of 512 balanced places. `segment_ids`: within each aligned block of 512 places the ids start at 0 and rise by one where a new sequence begins, so a block holds at most 8 sequences; in every draw some block holds a single sequence of 512 tokens and some block holds 8 sequences.
All inputs are finite; a program needn't handle non-finite values.
Results may differ from a plain program's by a relative error of at most 0.028.
Values may be sent and summed in bfloat16 or wider, within the bound.
No kernel may reach another device: no remote copies, remote signals or barrier semaphores. Data moves between devices by JAX's collectives and lax.ppermute only.
A program may use at most 128 MiB of HBM per device.

v0:
```python
from functools import partial
import jax
import jax.numpy as jnp
from jax import lax
from jax.sharding import PartitionSpec as P

HEADS = 32
KV = 4
HD = 64
EPS = 1e-05
ROPE_BASE = 10000.0


def rope_tables(positions):
    half_width = HD // 2
    freqs = ROPE_BASE ** (-(jnp.arange(half_width, dtype=jnp.float32) * 2.0 / HD))
    angles = positions.astype(jnp.float32)[:, None] * freqs[None, :]
    return (jnp.cos(angles)[:, None, :], jnp.sin(angles)[:, None, :])


def rotate(values, cosine, sine):
    half_width = values.shape[-1] // 2
    first = values[..., :half_width]
    second = values[..., half_width:]
    return jnp.concatenate(
        [first * cosine - second * sine, second * cosine + first * sine], axis=-1
    )


def rotate_back(grads, cosine, sine):
    half_width = grads.shape[-1] // 2
    first = grads[..., :half_width]
    second = grads[..., half_width:]
    return jnp.concatenate(
        [first * cosine + second * sine, second * cosine - first * sine], axis=-1
    )


def positions_of(segment_ids):
    index = jnp.arange(segment_ids.shape[0], dtype=jnp.int32)
    change = jnp.concatenate([jnp.ones((1,), dtype=jnp.bool_), segment_ids[1:] != segment_ids[:-1]])
    starts = jnp.where(change, index, jnp.zeros_like(index))
    return index - lax.cummax(starts, axis=0)


def allowed_pairs(segment_ids):
    index = jnp.arange(segment_ids.shape[0], dtype=jnp.int32)
    return (segment_ids[:, None] == segment_ids[None, :]) & (index[None, :] <= index[:, None])


def rms_scale(values):
    return lax.rsqrt(jnp.mean(values * values, axis=-1, keepdims=True) + EPS)


def norm_back(values, inv_root, gain, grads):
    normed = values * inv_root
    scaled = grads * gain
    result = inv_root * (scaled - normed * jnp.mean(scaled * normed, axis=-1, keepdims=True))
    return (result, jnp.sum(grads * normed, axis=0))


def matmul(left, right):
    return jnp.dot(left, right, preferred_element_type=jnp.float32)


def head_scores(query_head, key_head, allowed, scale_factor):
    scores = matmul(query_head, key_head.T) * scale_factor
    return jnp.where(allowed, scores, -1e30)


def head_forward(inputs, key_heads, value_heads, allowed, scale_factor):
    query_head, kv_slot = inputs
    scores = head_scores(query_head, key_heads[kv_slot], allowed, scale_factor)
    peak = jnp.max(scores, axis=-1, keepdims=True)
    expo = jnp.exp(scores - peak)
    total = jnp.sum(expo, axis=-1, keepdims=True)
    probs = expo / total
    mixed = matmul(probs.astype(jnp.bfloat16), value_heads[kv_slot])
    return (mixed, (peak + jnp.log(total))[:, 0])


def head_backward(inputs, key_heads, value_heads, allowed, scale_factor):
    query_head, kv_slot, grad_head, log_total = inputs
    key_head = key_heads[kv_slot]
    value_head = value_heads[kv_slot]
    scores = head_scores(query_head, key_head, allowed, scale_factor)
    probs = jnp.exp(scores - log_total[:, None])
    prob_grad = matmul(grad_head, value_head.T)
    value_grad = matmul(probs.astype(jnp.bfloat16).T, grad_head)
    inner = jnp.sum(probs * prob_grad, axis=-1, keepdims=True)
    score_grad = (probs * (prob_grad - inner)).astype(jnp.bfloat16)
    query_grad = matmul(score_grad, key_head) * scale_factor
    key_grad = matmul(score_grad.T, query_head) * scale_factor
    return (query_grad, key_grad, value_grad)


def body(
    tokens,
    cotangent,
    destination,
    segment_ids,
    attn_gain,
    w_query,
    w_key,
    w_value,
    w_output,
    ffn_gain,
    w_gate,
    w_up,
    w_down,
):
    row_count = tokens.shape[0]
    quarter = tokens.shape[1]
    col_start = lax.axis_index("col") * quarter
    group_size = HEADS // KV
    send_order = jnp.argsort(destination)
    slot_ids = destination[send_order] % row_count
    arrived_rows, arrived_grads, arrived_slots = (
        lax.all_to_all(tokens[send_order], "row", split_axis=0, concat_axis=0, tiled=True),
        lax.all_to_all(cotangent[send_order], "row", split_axis=0, concat_axis=0, tiled=True),
        lax.all_to_all(slot_ids, "row", split_axis=0, concat_axis=0, tiled=True),
    )
    placing = jnp.argsort(arrived_slots)
    full_rows, full_grads = (
        lax.all_gather(arrived_rows[placing], "col", axis=1, tiled=True),
        lax.all_gather(arrived_grads[placing], "col", axis=1, tiled=True),
    )
    query_w, key_w, value_w, output_w = (
        lax.all_gather(w_query, "row", axis=0, tiled=True),
        lax.all_gather(w_key, "row", axis=0, tiled=True),
        lax.all_gather(w_value, "row", axis=0, tiled=True),
        lax.all_gather(w_output, "row", axis=0, tiled=True),
    )
    cosine, sine = rope_tables(positions_of(segment_ids))
    allowed = allowed_pairs(segment_ids)
    rows_wide = full_rows.astype(jnp.float32)
    inv_one = rms_scale(rows_wide)
    normed_one = (rows_wide * inv_one * attn_gain).astype(jnp.bfloat16)
    query = matmul(normed_one, query_w)
    key_raw = matmul(normed_one, key_w)
    value_raw = matmul(normed_one, value_w)
    query_heads_count = query.shape[1] // HD
    kv_count = key_raw.shape[1] // HD
    query_rot = (
        rotate(query.reshape(row_count, query_heads_count, HD), cosine, sine)
        .astype(jnp.bfloat16)
        .transpose(1, 0, 2)
    )
    key_rot = (
        rotate(key_raw.reshape(row_count, kv_count, HD), cosine, sine)
        .astype(jnp.bfloat16)
        .transpose(1, 0, 2)
    )
    value_heads = value_raw.astype(jnp.bfloat16).reshape(row_count, kv_count, HD).transpose(1, 0, 2)
    kv_slots = jnp.arange(query_heads_count, dtype=jnp.int32) // group_size
    scale_factor = HD ** (-0.5)
    mixed_heads, log_totals = lax.map(
        partial(
            head_forward,
            key_heads=key_rot,
            value_heads=value_heads,
            allowed=allowed,
            scale_factor=scale_factor,
        ),
        (query_rot, kv_slots),
    )
    mixed = (
        mixed_heads.transpose(1, 0, 2)
        .reshape(row_count, query_heads_count * HD)
        .astype(jnp.bfloat16)
    )
    attn_terms = matmul(mixed, output_w.T)
    attn_full = lax.psum(attn_terms, "col")
    resid = rows_wide + attn_full
    inv_two = rms_scale(resid)
    normed_two = (resid * inv_two * ffn_gain).astype(jnp.bfloat16)
    resid_part = lax.dynamic_slice_in_dim(resid, col_start, quarter, 1)
    gate_w, up_w, down_w = (
        lax.all_gather(w_gate, "row", axis=0, tiled=True),
        lax.all_gather(w_up, "row", axis=0, tiled=True),
        lax.all_gather(w_down, "row", axis=0, tiled=True),
    )
    gate = matmul(normed_two, gate_w)
    upper = matmul(normed_two, up_w)
    sigmoid_gate = jax.nn.sigmoid(gate)
    activ = (gate * sigmoid_gate * upper).astype(jnp.bfloat16)
    ffn_share = lax.psum_scatter(
        matmul(activ, down_w.T).astype(jnp.bfloat16), "col", scatter_dimension=1, tiled=True
    ).astype(jnp.float32)
    output_share = (resid_part + ffn_share).astype(jnp.bfloat16)
    gate_w, up_w, down_w = (
        lax.all_gather(w_gate, "row", axis=0, tiled=True),
        lax.all_gather(w_up, "row", axis=0, tiled=True),
        lax.all_gather(w_down, "row", axis=0, tiled=True),
    )
    down_weight_grad = matmul(full_grads.T, activ)
    act_grad = matmul(full_grads, down_w)
    gate_grad = (act_grad * upper * sigmoid_gate * (1.0 + gate * (1.0 - sigmoid_gate))).astype(
        jnp.bfloat16
    )
    up_grad = (act_grad * gate * sigmoid_gate).astype(jnp.bfloat16)
    gate_weight_grad = matmul(normed_two.T, gate_grad)
    up_weight_grad = matmul(normed_two.T, up_grad)
    normed_terms_two = matmul(gate_grad, gate_w.T) + matmul(up_grad, up_w.T)
    normed_grad_two = lax.psum(normed_terms_two, "col")
    resid_norm_grad, ffn_gain_grad = norm_back(resid, inv_two, ffn_gain, normed_grad_two)
    resid_grad = full_grads.astype(jnp.float32) + resid_norm_grad
    attn_grad_low = resid_grad.astype(jnp.bfloat16)
    ffn_results = (
        lax.psum_scatter(
            gate_weight_grad.astype(jnp.bfloat16), "row", scatter_dimension=0, tiled=True
        ).astype(jnp.float32),
        lax.psum_scatter(
            up_weight_grad.astype(jnp.bfloat16), "row", scatter_dimension=0, tiled=True
        ).astype(jnp.float32),
        lax.psum_scatter(
            down_weight_grad.astype(jnp.bfloat16), "row", scatter_dimension=0, tiled=True
        ).astype(jnp.float32),
        lax.psum_scatter(
            ffn_gain_grad.astype(jnp.bfloat16), "row", scatter_dimension=0, tiled=True
        ).astype(jnp.float32),
    )
    query_w, key_w, value_w, output_w = (
        lax.all_gather(w_query, "row", axis=0, tiled=True),
        lax.all_gather(w_key, "row", axis=0, tiled=True),
        lax.all_gather(w_value, "row", axis=0, tiled=True),
        lax.all_gather(w_output, "row", axis=0, tiled=True),
    )
    output_weight_grad = matmul(attn_grad_low.T, mixed)
    mixed_grad = matmul(attn_grad_low, output_w).astype(jnp.bfloat16)
    mixed_grad_heads = mixed_grad.reshape(row_count, query_heads_count, HD).transpose(1, 0, 2)
    query_grads, key_grads, value_grads = lax.map(
        partial(
            head_backward,
            key_heads=key_rot,
            value_heads=value_heads,
            allowed=allowed,
            scale_factor=scale_factor,
        ),
        (query_rot, kv_slots, mixed_grad_heads, log_totals),
    )
    query_grad = (
        rotate_back(query_grads.transpose(1, 0, 2), cosine, sine)
        .reshape(row_count, query_heads_count * HD)
        .astype(jnp.bfloat16)
    )
    key_sum = key_grads.reshape(kv_count, group_size, row_count, HD).sum(axis=1).transpose(1, 0, 2)
    key_grad = (
        rotate_back(key_sum, cosine, sine).reshape(row_count, kv_count * HD).astype(jnp.bfloat16)
    )
    value_sum = (
        value_grads.reshape(kv_count, group_size, row_count, HD).sum(axis=1).transpose(1, 0, 2)
    )
    value_grad = value_sum.reshape(row_count, kv_count * HD).astype(jnp.bfloat16)
    query_weight_grad = matmul(normed_one.T, query_grad)
    key_weight_grad = matmul(normed_one.T, key_grad)
    value_weight_grad = matmul(normed_one.T, value_grad)
    normed_terms_one = (
        matmul(query_grad, query_w.T) + matmul(key_grad, key_w.T) + matmul(value_grad, value_w.T)
    )
    normed_grad_one = lax.psum(normed_terms_one.astype(jnp.bfloat16), "col").astype(jnp.float32)
    rows_norm_grad, attn_gain_grad = norm_back(rows_wide, inv_one, attn_gain, normed_grad_one)
    rows_grad = resid_grad + rows_norm_grad
    input_share = lax.dynamic_slice_in_dim(rows_grad, col_start, quarter, 1).astype(jnp.bfloat16)
    attn_results = (
        lax.psum_scatter(
            query_weight_grad.astype(jnp.bfloat16), "row", scatter_dimension=0, tiled=True
        ).astype(jnp.float32),
        lax.psum_scatter(
            key_weight_grad.astype(jnp.bfloat16), "row", scatter_dimension=0, tiled=True
        ).astype(jnp.float32),
        lax.psum_scatter(
            value_weight_grad.astype(jnp.bfloat16), "row", scatter_dimension=0, tiled=True
        ).astype(jnp.float32),
        lax.psum_scatter(
            output_weight_grad.astype(jnp.bfloat16), "row", scatter_dimension=0, tiled=True
        ).astype(jnp.float32),
        lax.psum_scatter(
            attn_gain_grad.astype(jnp.bfloat16), "row", scatter_dimension=0, tiled=True
        ).astype(jnp.float32),
    )
    back_rows, back_grads = (
        lax.all_to_all(output_share[arrived_slots], "row", split_axis=0, concat_axis=0, tiled=True),
        lax.all_to_all(input_share[arrived_slots], "row", split_axis=0, concat_axis=0, tiled=True),
    )
    restore = jnp.argsort(send_order)
    return (
        back_rows[restore],
        back_grads[restore],
        attn_results[4],
        attn_results[0],
        attn_results[1],
        attn_results[2],
        attn_results[3],
        ffn_results[3],
        ffn_results[0],
        ffn_results[1],
        ffn_results[2],
    )


def solution(mesh):
    placed = (
        P("row", "col"),
        P("row", "col"),
        P("row"),
        P("row"),
        P(),
        P("row", "col"),
        P("row", "col"),
        P("row", "col"),
        P("row", "col"),
        P(),
        P("row", "col"),
        P("row", "col"),
        P("row", "col"),
    )
    return jax.shard_map(
        body,
        mesh=mesh,
        in_specs=placed,
        out_specs=(
            P("row", "col"),
            P("row", "col"),
            P("row"),
            P("row", "col"),
            P("row", "col"),
            P("row", "col"),
            P("row", "col"),
            P("row"),
            P("row", "col"),
            P("row", "col"),
            P("row", "col"),
        ),
        check_vma=False,
    )
```

profile of v0, /device:TPU:0, one launch (start us, length us, event | category | flops | bytes accessed | tf_op | source)
XLA Modules:
  0.0 1312.7 jit_solution(15525933860058886407)
XLA Ops:
  16.6 8.4 all-to-all-start.1
  53.0 22.4 %all_gather.36 = bf16[2048,64]{1,0:T(8,128)(2,1)S(1)} all-gather(bf16[64,64]{1,0:T(8,128)(2,1)S(1)} %copy-done.22), channel_id=1, replica_groups=mesh['row'=32,'col'=4] {'row'}, dimensions={0}, use_global_device_ids=true | all-gather | bytes 270336 | tf_op jit(solution)/shard_map/all_gather | solution.py:130
  75.5 26.7 %all_gather.37 = bf16[2048,64]{1,0:T(8,128)(2,1)} all-gather(bf16[64,64]{1,0:T(8,128)(2,1)S(1)} %copy-done.23), channel_id=1, replica_groups=mesh['row'=32,'col'=4] {'row'}, dimensions={0}, use_global_device_ids=true | all-gather | bytes 270336 | tf_op jit(solution)/shard_map/all_gather | solution.py:131
  111.2 14.4 %all-gather.10.cloned.1.call-done = bf16[2048,512]{1,0:T(8,128)(2,1)} async-done(((bf16[64,512]{1,0:T(8,128)(2,1)}), bf16[2048,512]{1,0:T(8,128)(2,1)}) %all-gather.10.cloned.1.call-update) | async-done | bytes 2097168 | tf_op jit(solution)/shard_map/all_gather | solution.py:129
  129.4 24.0 %while.32 = (s32[]{:T(128)}, bf16[8,512,64]{1,2,0:T(8,128)(2,1)S(1)}, f32[8,512]{1,0:T(8,128)}, bf16[8,512,64]{2,1,0:T(8,128)(2,1)S(1)}, bf16[1,512,64]{2,1,0:T(...) while((s32[]{:T(128)}, bf16[8,512,64]{1,2,0:T(8,128)(2,1)S(1)}, ...), condition=%wide.region_8.9_spmd.clone.clone, body=%wide.region_5.8_spmd.clone.sunk.clone | while | flops 69991936 | bytes 3695189 | solution.py:157
  153.4 17.8 %all-gather.12.cloned.1.call-done = bf16[2048,512]{1,0:T(8,128)(2,1)} async-done(((bf16[64,512]{1,0:T(8,128)(2,1)}), bf16[2048,512]{1,0:T(8,128)(2,1)}) %all-gather.12.cloned.1.call-update) | async-done | bytes 2097168 | tf_op jit(solution)/shard_map/all_gather | solution.py:132
  180.0 17.1 %all_to_all.60 = bf16[32,16,512]{2,1,0:T(8,128)(2,1)S(1)} all-to-all(bf16[32,16,512]{2,1,0:T(8,128)(2,1)} %bitcast.194), channel_id=1, replica_groups=mesh['row'=32,'col'=4] {'row'}, dimensions={0} | all-to-all | bytes 1048576 | tf_op jit(solution)/shard_map/all_to_all | solution.py:120
  201.1 67.2 %all-reduce.7.cloned.1.call-done = f32[512,2048]{1,0:T(8,128)} async-done(((f32[512,2048]{1,0:T(8,128)}), f32[512,2048]{1,0:T(8,128)}) %all-reduce.7.cloned.1.call-update) | async-done | bytes 4194320 | tf_op jit(solution)/shard_map/psum | solution.py:173
  274.8 44.2 %all-gather.14.cloned.1.call-done = bf16[2048,1408]{1,0:T(8,128)(2,1)} async-done(((bf16[64,1408]{1,0:T(8,128)(2,1)}), bf16[2048,1408]{1,0:T(8,128)(2,1)}) %all-gather.14.cloned.1.call-update) | async-done | bytes 5767184 | tf_op jit(solution)/shard_map/all_gather | solution.py:179
  319.0 8.3 fusion.76
  327.3 41.5 %all-gather.16.cloned.1.call-done = bf16[2048,1408]{1,0:T(8,128)(2,1)} async-done(((bf16[64,1408]{1,0:T(8,128)(2,1)}), bf16[2048,1408]{1,0:T(8,128)(2,1)}) %all-gather.16.cloned.1.call-update) | async-done | bytes 5767184 | tf_op jit(solution)/shard_map/all_gather | solution.py:180
  368.8 8.3 fusion.77
  377.1 23.9 %all-gather.22.cloned.1.call-done = bf16[512,2048]{1,0:T(8,128)(2,1)} async-done(((bf16[512,512]{1,0:T(8,128)(2,1)}), bf16[512,2048]{1,0:T(8,128)(2,1)}) %all-gather.22.cloned.1.call-update) | async-done | bytes 2097168 | tf_op jit(solution)/shard_map/all_gather | solution.py:126
  400.9 51.0 %all-gather.18.cloned.1.call-done = bf16[2048,1408]{1,0:T(8,128)(2,1)} async-done(((bf16[64,1408]{1,0:T(8,128)(2,1)}), bf16[2048,1408]{1,0:T(8,128)(2,1)}) %all-gather.18.cloned.1.call-update) | async-done | bytes 5767184 | tf_op jit(solution)/shard_map/all_gather | solution.py:181
  452.0 10.3 multiply_convert_fusion.3
  474.2 7.9 convolution_convert_fusion.5
  482.2 83.7 %all-reduce.9.cloned.1.call-done = f32[512,2048]{1,0:T(8,128)} async-done(((f32[512,2048]{1,0:T(8,128)}), f32[512,2048]{1,0:T(8,128)}) %all-reduce.9.cloned.1.call-update) | async-done | bytes 4194320 | tf_op jit(solution)/shard_map/psum | solution.py:205
  579.3 65.5 %while.33 = (s32[]{:T(128)}, f32[8,512,64]{1,2,0:T(8,128)}, f32[8,512,64]{1,2,0:T(8,128)}, f32[8,512,64]{1,2,0:T(8,128)}, bf16[8,512,64]{2,1,0:T(8,128)(2,1)}, /...) while((s32[]{:T(128)}, f32[8,512,64]{1,2,0:T(8,128)}, ...), condition=%wide.region_17.18_spmd.clone.clone, body=%wide.region_15.17_spmd.clone.sunk.clone | while | flops 170982912 | bytes 8996457 | solution.py:232
  667.5 8.0 convolution_convert_fusion.2
  675.5 8.1 convolution_convert_fusion.1
  683.9 7.9 convolution_convert_fusion
  696.3 7.3 all-to-all-start.2
  703.5 10.4 all-reduce.11.cloned.1.call-done
  721.0 7.3 all-to-all-start.4
  733.4 61.5 %reduce-scatter.13.cloned.1.call-done = bf16[64,64]{1,0:T(8,128)(2,1)} async-done(((bf16[2048,64]{1,0:T(8,128)(2,1)}), bf16[64,64]{1,0:T(8,128)(2,1)}) %reduce-scatter.13.cloned.1.call-update) | async-done | bytes 8208 | tf_op jit(solution)/shard_map/reduce_scatter | solution.py:269
  796.2 78.5 %reduce-scatter.15.cloned.1.call-done = bf16[64,64]{1,0:T(8,128)(2,1)} async-done(((bf16[2048,64]{1,0:T(8,128)(2,1)}), bf16[64,64]{1,0:T(8,128)(2,1)}) %reduce-scatter.15.cloned.1.call-update) | async-done | bytes 8208 | tf_op jit(solution)/shard_map/reduce_scatter | solution.py:272
  878.7 64.4 %all-reduce.2 = (bf16[2048]{0:T(1024)(128)(2,1)S(1)}, bf16[2048]{0:T(1024)(128)(2,1)S(1)}) all-reduce(bf16[2048]{0:T(1024)(128)(2,1)S(1)} %get-tuple-element.249, bf16[2048]{0:T(1024)(128)(2,1)S(1)} %copy-done.20), channel_id=5, replica_groups=mesh['row'=32,'col'=4] {'row'}, use_global_device_ids=true, to_apply=%region_23.24.clone | all-reduce | flops 4096 | bytes 16384
  946.4 10.0 reduce-scatter.11.cloned.1.call-done
  957.9 80.2 %reduce-scatter.17.cloned.1.call-done = bf16[64,512]{1,0:T(8,128)(2,1)} async-done(((bf16[2048,512]{1,0:T(8,128)(2,1)}), bf16[64,512]{1,0:T(8,128)(2,1)}) %reduce-scatter.17.cloned.1.call-update) | async-done | bytes 65552 | tf_op jit(solution)/shard_map/reduce_scatter | solution.py:275
  1039.6 86.9 %reduce-scatter.19.cloned.1.call-done = bf16[64,1408]{1,0:T(8,128)(2,1)} async-done(((bf16[2048,1408]{1,0:T(8,128)(2,1)}), bf16[64,1408]{1,0:T(8,128)(2,1)}) %reduce-scatter.19.cloned.1.call-update) | async-done | bytes 180240 | tf_op jit(solution)/shard_map/reduce_scatter | solution.py:210
  1128.2 87.2 %reduce-scatter.21.cloned.1.call-done = bf16[64,1408]{1,0:T(8,128)(2,1)} async-done(((bf16[2048,1408]{1,0:T(8,128)(2,1)}), bf16[64,1408]{1,0:T(8,128)(2,1)}) %reduce-scatter.21.cloned.1.call-update) | async-done | bytes 180240 | tf_op jit(solution)/shard_map/reduce_scatter | solution.py:213
  1217.0 86.7 %reduce-scatter.23.cloned.1.call-done = bf16[64,1408]{1,0:T(8,128)(2,1)} async-done(((bf16[2048,1408]{1,0:T(8,128)(2,1)}), bf16[64,1408]{1,0:T(8,128)(2,1)}) %reduce-scatter.23.cloned.1.call-update) | async-done | bytes 180240 | tf_op jit(solution)/shard_map/reduce_scatter | solution.py:216
  (298 shorter events, 239.0 us)
Async XLA Ops:
  16.6 15.7 %all-to-all-start.1 = ((s32[32,16,1]{1,2,0:T(1,128)}), s32[32,16,1]{1,2,0:T(1,128)S(1)}, u32[]{:S(2)}, u32[]{:S(2)}) async-start(s32[32,16,1]{1,2,0:T(1,128)} %bitcast.2), calls=%async_computation.1 | async-start | bytes 32768 | tf_op jit(solution)/shard_map/all_to_all | solution.py:121
  27.7 25.3 %copy-start.22 = (bf16[64,64]{1,0:T(8,128)(2,1)S(1)}, bf16[64,64]{1,0:T(8,128)(2,1)}, u32[]{:S(2)}) copy-start(bf16[64,64]{1,0:T(8,128)(2,1)} %param.23) | copy-start | bytes 24580
  27.7 47.8 %copy-start.23 = (bf16[64,64]{1,0:T(8,128)(2,1)S(1)}, bf16[64,64]{1,0:T(8,128)(2,1)}, u32[]{:S(2)}) copy-start(bf16[64,64]{1,0:T(8,128)(2,1)} %param.24) | copy-start | bytes 24580
  32.3 15.7 %all-to-all-start = ((bf16[32,16,512]{2,1,0:T(8,128)(2,1)}), bf16[32,16,512]{2,1,0:T(8,128)(2,1)S(1)}, u32[]{:S(2)}, u32[]{:S(2)}) async-start(bf16[32,16,512]{2,1,0:T(8,128)(2,1)} %bitcast), calls=%async_computation | async-start | bytes 1048576 | tf_op jit(solution)/shard_map/all_to_all | solution.py:119
  36.2 66.3 %all-gather.20.cloned.1.call-start = ((), (), s32[]{:S(2)}) async-start(), calls=%async_computation.29 | async-start | bytes 2621440 | tf_op jit(solution)/shard_map/all_gather | solution.py:125
  48.0 56.8 %copy-start.24 = (f32[2048]{0:T(1024)S(1)}, f32[2048]{0:T(1024)}, u32[]{:S(2)}) copy-start(f32[2048]{0:T(1024)} %param.21) | copy-start | bytes 24580
  50.6 75.0 %all-gather.10.cloned.1.call-start = ((), (), s32[]{:S(2)}) async-start(), calls=%async_computation.13 | async-start | bytes 2162688 | tf_op jit(solution)/shard_map/all_gather | solution.py:129
  51.4 119.8 %all-gather.12.cloned.1.call-start = ((), (), s32[]{:S(2)}) async-start(), calls=%async_computation.14 | async-start | bytes 2162688 | tf_op jit(solution)/shard_map/all_gather | solution.py:132
  52.1 216.2 %all-reduce.7.cloned.1.call-start = ((), (), s32[]{:S(2)}) async-start(), calls=%async_computation.15 | async-start | bytes 8388608 | tf_op jit(solution)/shard_map/psum | solution.py:173
  52.2 55.4 %copy-start.29 = (f32[32]{0:T(128)}, f32[32]{0:T(128)S(1)}, u32[]{:S(2)}) copy-start(f32[32]{0:T(128)S(1)} %negate_power_fusion) | copy-start | bytes 388
  53.0 54.5 %copy-start.15 = (f32[512]{0:T(512)}, f32[512]{0:T(512)S(1)}, u32[]{:S(2)}) copy-start(f32[512]{0:T(512)S(1)} %fusion.70) | copy-start | bytes 6148
  75.5 34.8 %copy-start.10 = (bf16[2048,64]{1,0:T(8,128)(2,1)}, bf16[2048,64]{1,0:T(8,128)(2,1)S(1)}, u32[]{:S(2)}) copy-start(bf16[2048,64]{1,0:T(8,128)(2,1)S(1)} %all_gather.36) | copy-start | bytes 786436
  176.1 142.8 %all-gather.14.cloned.1.call-start = ((), (), s32[]{:S(2)}) async-start(), calls=%async_computation.16 | async-start | bytes 5947392 | tf_op jit(solution)/shard_map/all_gather | solution.py:179
  176.7 192.1 %all-gather.16.cloned.1.call-start = ((), (), s32[]{:S(2)}) async-start(), calls=%async_computation.17 | async-start | bytes 5947392 | tf_op jit(solution)/shard_map/all_gather | solution.py:180
  177.3 223.6 %all-gather.22.cloned.1.call-start = ((), (), s32[]{:S(2)}) async-start(), calls=%async_computation.30 | async-start | bytes 2621440 | tf_op jit(solution)/shard_map/all_gather | solution.py:126
  180.0 88.3 %copy-start.7 = (bf16[512,2048]{1,0:T(8,128)(2,1)S(1)}, bf16[512,2048]{1,0:T(8,128)(2,1)}, u32[]{:S(2)}) copy-start(bf16[512,2048]{1,0:T(8,128)(2,1)} %all-gather.20.cloned.1.call-done) | copy-start | bytes 6291460
  199.9 252.1 %all-gather.18.cloned.1.call-start = ((), (), s32[]{:S(2)}) async-start(), calls=%async_computation.18 | async-start | bytes 5947392 | tf_op jit(solution)/shard_map/all_gather | solution.py:181
  200.6 72.4 %copy-start.14 = (f32[2048]{0:T(1024)S(1)}, f32[2048]{0:T(1024)}, u32[]{:S(2)}) copy-start(f32[2048]{0:T(1024)} %param.26) | copy-start | bytes 24580
  200.6 365.2 %all-reduce.9.cloned.1.call-start = ((), (), s32[]{:S(2)}) async-start(), calls=%async_computation.20 | async-start | bytes 8388608 | tf_op jit(solution)/shard_map/psum | solution.py:205
  474.0 218.0 %reduce-scatter.9.cloned.1.call-start = ((), (), s32[]{:S(2)}) async-start(), calls=%async_computation.19 | async-start | bytes 2621440 | tf_op jit(solution)/shard_map/reduce_scatter | solution.py:187
  482.1 231.8 %all-reduce.11.cloned.1.call-start = ((), (), s32[]{:S(2)}) async-start(), calls=%async_computation.21 | async-start | bytes 4194304 | tf_op jit(solution)/shard_map/psum | solution.py:261
  655.2 139.7 %reduce-scatter.13.cloned.1.call-start = ((), (), s32[]{:S(2)}) async-start(), calls=%async_computation.23 | async-start | bytes 540672 | tf_op jit(solution)/shard_map/reduce_scatter | solution.py:269
  657.1 217.6 %reduce-scatter.15.cloned.1.call-start = ((), (), s32[]{:S(2)}) async-start(), calls=%async_computation.24 | async-start | bytes 540672 | tf_op jit(solution)/shard_map/reduce_scatter | solution.py:272
  659.2 297.1 %reduce-scatter.11.cloned.1.call-start = ((), (), s32[]{:S(2)}) async-start(), calls=%async_computation.22 | async-start | bytes 2162688 | tf_op jit(solution)/shard_map/reduce_scatter | solution.py:266
  662.1 375.9 %reduce-scatter.17.cloned.1.call-start = ((), (), s32[]{:S(2)}) async-start(), calls=%async_computation.25 | async-start | bytes 2162688 | tf_op jit(solution)/shard_map/reduce_scatter | solution.py:275
  667.4 459.0 %reduce-scatter.19.cloned.1.call-start = ((), (), s32[]{:S(2)}) async-start(), calls=%async_computation.26 | async-start | bytes 5947392 | tf_op jit(solution)/shard_map/reduce_scatter | solution.py:210
  675.5 539.8 %reduce-scatter.21.cloned.1.call-start = ((), (), s32[]{:S(2)}) async-start(), calls=%async_computation.27 | async-start | bytes 5947392 | tf_op jit(solution)/shard_map/reduce_scatter | solution.py:213
  683.6 620.1 %reduce-scatter.23.cloned.1.call-start = ((), (), s32[]{:S(2)}) async-start(), calls=%async_computation.28 | async-start | bytes 5947392 | tf_op jit(solution)/shard_map/reduce_scatter | solution.py:216
  696.3 24.8 %all-to-all-start.2 = ((bf16[32,16,512]{2,1,0:T(8,128)(2,1)}), bf16[32,16,512]{2,1,0:T(8,128)(2,1)S(1)}, u32[]{:S(2)}, u32[]{:S(2)}) async-start(bf16[32,16,512]{2,1,0:T(8,128)(2,1)} %bitcast.14), calls=%async_computation.3 | async-start | bytes 1048576 | tf_op jit(solution)/shard_map/all_to_all | solution.py:283
  718.4 160.3 %copy-start.20 = (bf16[2048]{0:T(1024)(128)(2,1)S(1)}, bf16[2048]{0:T(1024)(128)(2,1)}, u32[]{:S(2)}) copy-start(bf16[2048]{0:T(1024)(128)(2,1)} %get-tuple-element.247) | copy-start | bytes 12292
  721.0 222.7 %all-to-all-start.4 = ((bf16[32,16,512]{2,1,0:T(8,128)(2,1)}), bf16[32,16,512]{2,1,0:T(8,128)(2,1)S(1)}, u32[]{:S(2)}, u32[]{:S(2)}) async-start(bf16[32,16,512]{2,1,0:T(8,128)(2,1)} %bitcast.24), calls=%async_computation.5 | async-start | bytes 1048576 | tf_op jit(solution)/shard_map/all_to_all | solution.py:284
  876.1 429.3 %copy-start.1 = (bf16[512,512]{1,0:T(8,128)(2,1)S(1)}, bf16[512,512]{1,0:T(8,128)(2,1)}, u32[]{:S(2)}) copy-start(bf16[512,512]{1,0:T(8,128)(2,1)} %param.17) | copy-start | bytes 1572868
  (24 other events, 188.3 us)
Sparse Core Ops, SparseCore 0:
  50.7 28.4 all-gather.19
  81.5 44.0 all-gather.9
  127.9 43.2 all-gather.11
  176.2 91.9 all-reduce.6
  270.6 48.3 all-gather.13
  321.3 47.4 all-gather.15
  371.1 29.7 all-gather.21
  403.4 48.4 all-gather.17
  474.1 91.7 all-reduce.8
  568.1 29.5 reduce-scatter.8
  655.3 58.5 all-reduce.10
  717.8 77.0 reduce-scatter.12
  798.4 76.3 reduce-scatter.14
  878.2 78.1 reduce-scatter.10
  959.8 78.2 reduce-scatter.16
  1041.7 84.7 reduce-scatter.18
  1130.5 84.7 reduce-scatter.20
  1218.9 84.7 reduce-scatter.22
where the time goes:
time: 1320 us; the launch traced here: 1310 us
  waiting for transfers between devices  860 us (65%)
  matrix products  170 us (13%)
  blocking collectives  131 us (10%)
  other arithmetic  55.9 us (4%)
  local copies, waits for them, and re-layouts  51.2 us (4%)
  starting transfers between devices  28.6 us (2%)
  between operations  16 us (1%)
    dot_general x77, matrix products, matmul(): return jnp.dot(left, right, preferred_element_type=jnp.float32)  170 us
    reduce_scatter x1, waiting for transfers between devices, body(): lax.psum_scatter(up_weight_grad.astype(jnp.bfloat16), 'row', scatter_dime...  87.2 us
    reduce_scatter x1, waiting for transfers between devices, body(): lax.psum_scatter(gate_weight_grad.astype(jnp.bfloat16), 'row', scatter_di...  86.9 us
    reduce_scatter x1, waiting for transfers between devices, body(): lax.psum_scatter(down_weight_grad.astype(jnp.bfloat16), 'row', scatter_di...  86.7 us
    psum x1, waiting for transfers between devices, body(): normed_grad_two = lax.psum(normed_terms_two, 'col')  83.7 us
    reduce_scatter x1, waiting for transfers between devices, body(): lax.psum_scatter(output_weight_grad.astype(jnp.bfloat16), 'row', scatter_...  80.2 us
    reduce_scatter x1, waiting for transfers between devices, body(): lax.psum_scatter(value_weight_grad.astype(jnp.bfloat16), 'row', scatter_d...  78.5 us
    psum x1, waiting for transfers between devices, body(): attn_full = lax.psum(attn_terms, 'col')  67.2 us
  transfers between devices with their start and end apart: 22, of which 18 were waited for; matrix products, arithmetic and copies ran while one was open for 18% of the time, Pallas kernels for 0%

commit v1 on v0

--- a/solution.py
+++ b/solution.py
@@ -170,7 +170,7 @@
         .astype(jnp.bfloat16)
     )
     attn_terms = matmul(mixed, output_w.T)
-    attn_full = lax.psum(attn_terms, "col")
+    attn_full = jnp.sum(lax.all_gather(attn_terms, "col"), axis=0)
     resid = rows_wide + attn_full
     inv_two = rms_scale(resid)
     normed_two = (resid * inv_two * ffn_gain).astype(jnp.bfloat16)

time: 1320 us -> 1380 us (1.045)
  waiting for transfers between devices: 860 us -> 914 us
    all_gather x0 -> x1, waiting for transfers between devices: none -> 130 us  [body(): attn_full = jnp.sum(lax.all_gather(attn_terms, 'col'), axis=0)]
    psum x1 -> x0, waiting for transfers between devices: 67.2 us -> none  [body(): attn_full = lax.psum(attn_terms, 'col')]
where the time goes in v1:
time: 1380 us
  waiting for transfers between devices  914 us (66%)
  matrix products  171 us (12%)
  blocking collectives  130 us (9%)
  other arithmetic  66.4 us (5%)
  local copies, waits for them, and re-layouts  50.4 us (4%)
  starting transfers between devices  28.2 us (2%)
  between operations  15.8 us (1%)
    dot_general x77, matrix products, matmul(): return jnp.dot(left, right, preferred_element_type=jnp.float32)  171 us
    all_gather x1, waiting for transfers between devices, body(): attn_full = jnp.sum(lax.all_gather(attn_terms, 'col'), axis=0)  130 us
    reduce_scatter x1, waiting for transfers between devices, body(): lax.psum_scatter(gate_weight_grad.astype(jnp.bfloat16), 'row', scatter_di...  87.4 us
    reduce_scatter x1, waiting for transfers between devices, body(): lax.psum_scatter(down_weight_grad.astype(jnp.bfloat16), 'row', scatter_di...  87.1 us
    reduce_scatter x1, waiting for transfers between devices, body(): lax.psum_scatter(up_weight_grad.astype(jnp.bfloat16), 'row', scatter_dime...  86.6 us
    psum x1, waiting for transfers between devices, body(): normed_grad_two = lax.psum(normed_terms_two, 'col')  83.9 us
    reduce_scatter x1, waiting for transfers between devices, body(): lax.psum_scatter(output_weight_grad.astype(jnp.bfloat16), 'row', scatter_...  80.6 us
    reduce_scatter x1, waiting for transfers between devices, body(): lax.psum_scatter(value_weight_grad.astype(jnp.bfloat16), 'row', scatter_d...  78.9 us
  transfers between devices with their start and end apart: 22, of which 18 were waited for; matrix products, arithmetic and copies ran while one was open for 18% of the time, Pallas kernels for 0%

profile of v1, /device:TPU:0, one launch (start us, length us, event | category | flops | bytes accessed | tf_op | source)
XLA Modules:
  0.0 1376.3 jit_solution(3324863743826475022)
XLA Ops:
  16.6 8.4 all-to-all-start.1
  53.0 22.4 %all_gather.42 = bf16[2048,64]{1,0:T(8,128)(2,1)S(1)} all-gather(bf16[64,64]{1,0:T(8,128)(2,1)S(1)} %copy-done.23), channel_id=1, replica_groups=mesh['row'=32,'col'=4] {'row'}, dimensions={0}, use_global_device_ids=true | all-gather | bytes 270336 | tf_op jit(solution)/shard_map/all_gather | solution.py:130
  75.5 26.7 %all_gather.43 = bf16[2048,64]{1,0:T(8,128)(2,1)} all-gather(bf16[64,64]{1,0:T(8,128)(2,1)S(1)} %copy-done.24), channel_id=1, replica_groups=mesh['row'=32,'col'=4] {'row'}, dimensions={0}, use_global_device_ids=true | all-gather | bytes 270336 | tf_op jit(solution)/shard_map/all_gather | solution.py:131
  111.2 14.5 %all-gather.12.cloned.1.call-done = bf16[2048,512]{1,0:T(8,128)(2,1)} async-done(((bf16[64,512]{1,0:T(8,128)(2,1)}), bf16[2048,512]{1,0:T(8,128)(2,1)}) %all-gather.12.cloned.1.call-update) | async-done | bytes 2097168 | tf_op jit(solution)/shard_map/all_gather | solution.py:129
  129.4 24.0 %while.32 = (s32[]{:T(128)}, bf16[8,512,64]{1,2,0:T(8,128)(2,1)S(1)}, f32[8,512]{1,0:T(8,128)}, bf16[8,512,64]{2,1,0:T(8,128)(2,1)S(1)}, bf16[1,512,64]{2,1,0:T(...) while((s32[]{:T(128)}, bf16[8,512,64]{1,2,0:T(8,128)(2,1)S(1)}, ...), condition=%wide.region_8.9_spmd.clone.clone, body=%wide.region_5.8_spmd.clone.sunk.clone | while | flops 69991936 | bytes 3695189 | solution.py:157
  153.4 17.8 %all-gather.14.cloned.1.call-done = bf16[2048,512]{1,0:T(8,128)(2,1)} async-done(((bf16[64,512]{1,0:T(8,128)(2,1)}), bf16[2048,512]{1,0:T(8,128)(2,1)}) %all-gather.14.cloned.1.call-update) | async-done | bytes 2097168 | tf_op jit(solution)/shard_map/all_gather | solution.py:132
  179.4 16.8 %all_to_all.60 = bf16[32,16,512]{2,1,0:T(8,128)(2,1)S(1)} all-to-all(bf16[32,16,512]{2,1,0:T(8,128)(2,1)S(1)} %bitcast.197), channel_id=1, replica_groups=mesh['row'=32,'col'=4] {'row'}, dimensions={0} | all-to-all | bytes 1048576 | tf_op jit(solution)/shard_map/all_to_all | solution.py:120
  199.8 129.8 %all-gather.24.cloned.1.call-done = f32[2048,2048]{1,0:T(8,128)} async-done(((f32[512,2048]{1,0:T(8,128)}), f32[2048,2048]{1,0:T(8,128)}) %all-gather.24.cloned.1.call-update) | async-done | bytes 16777232 | tf_op jit(solution)/shard_map/all_gather | solution.py:173
  329.6 10.4 reduce_sum.102
  346.7 34.4 %all-gather.16.cloned.1.call-done = bf16[2048,1408]{1,0:T(8,128)(2,1)} async-done(((bf16[64,1408]{1,0:T(8,128)(2,1)}), bf16[2048,1408]{1,0:T(8,128)(2,1)}) %all-gather.16.cloned.1.call-update) | async-done | bytes 5767184 | tf_op jit(solution)/shard_map/all_gather | solution.py:179
  381.2 8.3 fusion.76
  389.4 41.3 %all-gather.18.cloned.1.call-done = bf16[2048,1408]{1,0:T(8,128)(2,1)} async-done(((bf16[64,1408]{1,0:T(8,128)(2,1)}), bf16[2048,1408]{1,0:T(8,128)(2,1)}) %all-gather.18.cloned.1.call-update) | async-done | bytes 5767184 | tf_op jit(solution)/shard_map/all_gather | solution.py:180
  430.7 8.3 fusion.77
  439.1 23.7 %all-gather.26.cloned.1.call-done = bf16[512,2048]{1,0:T(8,128)(2,1)} async-done(((bf16[512,512]{1,0:T(8,128)(2,1)}), bf16[512,2048]{1,0:T(8,128)(2,1)}) %all-gather.26.cloned.1.call-update) | async-done | bytes 2097168 | tf_op jit(solution)/shard_map/all_gather | solution.py:126
  462.8 50.8 %all-gather.20.cloned.1.call-done = bf16[2048,1408]{1,0:T(8,128)(2,1)} async-done(((bf16[64,1408]{1,0:T(8,128)(2,1)}), bf16[2048,1408]{1,0:T(8,128)(2,1)}) %all-gather.20.cloned.1.call-update) | async-done | bytes 5767184 | tf_op jit(solution)/shard_map/all_gather | solution.py:181
  513.6 10.3 multiply_convert_fusion.3
  536.1 7.8 convolution_convert_fusion.5
  544.1 83.9 %all-reduce.6.cloned.1.call-done = f32[512,2048]{1,0:T(8,128)} async-done(((f32[512,2048]{1,0:T(8,128)}), f32[512,2048]{1,0:T(8,128)}) %all-reduce.6.cloned.1.call-update) | async-done | bytes 4194320 | tf_op jit(solution)/shard_map/psum | solution.py:205
  641.3 65.5 %while.33 = (s32[]{:T(128)}, f32[8,512,64]{1,2,0:T(8,128)}, f32[8,512,64]{1,2,0:T(8,128)}, f32[8,512,64]{1,2,0:T(8,128)}, bf16[8,512,64]{2,1,0:T(8,128)(2,1)}, /...) while((s32[]{:T(128)}, f32[8,512,64]{1,2,0:T(8,128)}, ...), condition=%wide.region_17.18_spmd.clone.clone, body=%wide.region_15.17_spmd.clone.sunk.clone | while | flops 170982912 | bytes 8996457 | solution.py:232
  729.7 8.0 convolution_convert_fusion.2
  737.8 8.1 convolution_convert_fusion.1
  745.9 7.9 convolution_convert_fusion
  758.3 7.5 all-to-all-start.2
  765.8 10.2 all-reduce.8.cloned.1.call-done
  795.4 61.9 %reduce-scatter.13.cloned.1.call-done = bf16[64,64]{1,0:T(8,128)(2,1)} async-done(((bf16[2048,64]{1,0:T(8,128)(2,1)}), bf16[64,64]{1,0:T(8,128)(2,1)}) %reduce-scatter.13.cloned.1.call-update) | async-done | bytes 8208 | tf_op jit(solution)/shard_map/reduce_scatter | solution.py:269
  858.7 78.9 %reduce-scatter.15.cloned.1.call-done = bf16[64,64]{1,0:T(8,128)(2,1)} async-done(((bf16[2048,64]{1,0:T(8,128)(2,1)}), bf16[64,64]{1,0:T(8,128)(2,1)}) %reduce-scatter.15.cloned.1.call-update) | async-done | bytes 8208 | tf_op jit(solution)/shard_map/reduce_scatter | solution.py:272
  941.5 64.4 %all-reduce.2 = (bf16[2048]{0:T(1024)(128)(2,1)S(1)}, bf16[2048]{0:T(1024)(128)(2,1)S(1)}) all-reduce(bf16[2048]{0:T(1024)(128)(2,1)S(1)} %get-tuple-element.249, bf16[2048]{0:T(1024)(128)(2,1)S(1)} %copy-done.20), channel_id=6, replica_groups=mesh['row'=32,'col'=4] {'row'}, use_global_device_ids=true, to_apply=%region_23.24.clone | all-reduce | flops 4096 | bytes 16384
  1009.1 10.4 reduce-scatter.11.cloned.1.call-done
  1021.0 80.6 %reduce-scatter.17.cloned.1.call-done = bf16[64,512]{1,0:T(8,128)(2,1)} async-done(((bf16[2048,512]{1,0:T(8,128)(2,1)}), bf16[64,512]{1,0:T(8,128)(2,1)}) %reduce-scatter.17.cloned.1.call-update) | async-done | bytes 65552 | tf_op jit(solution)/shard_map/reduce_scatter | solution.py:275
  1103.1 87.4 %reduce-scatter.19.cloned.1.call-done = bf16[64,1408]{1,0:T(8,128)(2,1)} async-done(((bf16[2048,1408]{1,0:T(8,128)(2,1)}), bf16[64,1408]{1,0:T(8,128)(2,1)}) %reduce-scatter.19.cloned.1.call-update) | async-done | bytes 180240 | tf_op jit(solution)/shard_map/reduce_scatter | solution.py:210
  1192.2 86.6 %reduce-scatter.21.cloned.1.call-done = bf16[64,1408]{1,0:T(8,128)(2,1)} async-done(((bf16[2048,1408]{1,0:T(8,128)(2,1)}), bf16[64,1408]{1,0:T(8,128)(2,1)}) %reduce-scatter.21.cloned.1.call-update) | async-done | bytes 180240 | tf_op jit(solution)/shard_map/reduce_scatter | solution.py:213
  1280.4 87.1 %reduce-scatter.23.cloned.1.call-done = bf16[64,1408]{1,0:T(8,128)(2,1)} async-done(((bf16[2048,1408]{1,0:T(8,128)(2,1)}), bf16[64,1408]{1,0:T(8,128)(2,1)}) %reduce-scatter.23.cloned.1.call-update) | async-done | bytes 180240 | tf_op jit(solution)/shard_map/reduce_scatter | solution.py:216
  (301 shorter events, 245.6 us)
Async XLA Ops:
  12.3 38.3 %copy-start.16 = (s32[1024]{0:T(1024)}, s32[1024]{0:T(1024)S(1)}, u32[]{:S(2)}) copy-start(s32[1024]{0:T(1024)S(1)} %pad_clamp_fusion.3) | copy-start | bytes 12292
  16.6 15.7 %all-to-all-start.1 = ((s32[32,16,1]{1,2,0:T(1,128)}), s32[32,16,1]{1,2,0:T(1,128)S(1)}, u32[]{:S(2)}, u32[]{:S(2)}) async-start(s32[32,16,1]{1,2,0:T(1,128)} %bitcast.2), calls=%async_computation.1 | async-start | bytes 32768 | tf_op jit(solution)/shard_map/all_to_all | solution.py:121
  27.7 25.3 %copy-start.23 = (bf16[64,64]{1,0:T(8,128)(2,1)S(1)}, bf16[64,64]{1,0:T(8,128)(2,1)}, u32[]{:S(2)}) copy-start(bf16[64,64]{1,0:T(8,128)(2,1)} %param.23) | copy-start | bytes 24580
  27.7 47.8 %copy-start.24 = (bf16[64,64]{1,0:T(8,128)(2,1)S(1)}, bf16[64,64]{1,0:T(8,128)(2,1)}, u32[]{:S(2)}) copy-start(bf16[64,64]{1,0:T(8,128)(2,1)} %param.24) | copy-start | bytes 24580
  32.3 15.7 %all-to-all-start = ((bf16[32,16,512]{2,1,0:T(8,128)(2,1)}), bf16[32,16,512]{2,1,0:T(8,128)(2,1)S(1)}, u32[]{:S(2)}, u32[]{:S(2)}) async-start(bf16[32,16,512]{2,1,0:T(8,128)(2,1)} %bitcast), calls=%async_computation | async-start | bytes 1048576 | tf_op jit(solution)/shard_map/all_to_all | solution.py:119
  36.2 66.3 %all-gather.22.cloned.1.call-start = ((), (), s32[]{:S(2)}) async-start(), calls=%async_computation.28 | async-start | bytes 2621440 | tf_op jit(solution)/shard_map/all_gather | solution.py:125
  41.3 61.1 %copy-start.21 = (s32[1024]{0:T(1024)}, s32[1024]{0:T(1024)S(1)}, u32[]{:S(2)}) copy-start(s32[1024]{0:T(1024)S(1)} %pad_clamp_fusion.2) | copy-start | bytes 12292
  48.0 56.7 %copy-start.25 = (f32[2048]{0:T(1024)S(1)}, f32[2048]{0:T(1024)}, u32[]{:S(2)}) copy-start(f32[2048]{0:T(1024)} %param.21) | copy-start | bytes 24580
  50.6 75.0 %all-gather.12.cloned.1.call-start = ((), (), s32[]{:S(2)}) async-start(), calls=%async_computation.13 | async-start | bytes 2162688 | tf_op jit(solution)/shard_map/all_gather | solution.py:129
  51.4 119.8 %all-gather.14.cloned.1.call-start = ((), (), s32[]{:S(2)}) async-start(), calls=%async_computation.14 | async-start | bytes 2162688 | tf_op jit(solution)/shard_map/all_gather | solution.py:132
  52.1 277.5 %all-gather.24.cloned.1.call-start = ((), (), s32[]{:S(2)}) async-start(), calls=%async_computation.29 | async-start | bytes 20971520 | tf_op jit(solution)/shard_map/all_gather | solution.py:173
  52.2 55.3 %copy-start.30 = (f32[32]{0:T(128)}, f32[32]{0:T(128)S(1)}, u32[]{:S(2)}) copy-start(f32[32]{0:T(128)S(1)} %negate_power_fusion) | copy-start | bytes 388
  53.0 54.5 %copy-start.15 = (f32[512]{0:T(512)}, f32[512]{0:T(512)S(1)}, u32[]{:S(2)}) copy-start(f32[512]{0:T(512)S(1)} %fusion.70) | copy-start | bytes 6148
  75.5 34.8 %copy-start.10 = (bf16[2048,64]{1,0:T(8,128)(2,1)}, bf16[2048,64]{1,0:T(8,128)(2,1)S(1)}, u32[]{:S(2)}) copy-start(bf16[2048,64]{1,0:T(8,128)(2,1)S(1)} %all_gather.42) | copy-start | bytes 786436
  176.2 205.0 %all-gather.16.cloned.1.call-start = ((), (), s32[]{:S(2)}) async-start(), calls=%async_computation.15 | async-start | bytes 5947392 | tf_op jit(solution)/shard_map/all_gather | solution.py:179
  176.8 254.0 %all-gather.18.cloned.1.call-start = ((), (), s32[]{:S(2)}) async-start(), calls=%async_computation.16 | async-start | bytes 5947392 | tf_op jit(solution)/shard_map/all_gather | solution.py:180
  177.3 285.5 %all-gather.26.cloned.1.call-start = ((), (), s32[]{:S(2)}) async-start(), calls=%async_computation.30 | async-start | bytes 2621440 | tf_op jit(solution)/shard_map/all_gather | solution.py:126
  198.8 314.7 %all-gather.20.cloned.1.call-start = ((), (), s32[]{:S(2)}) async-start(), calls=%async_computation.17 | async-start | bytes 5947392 | tf_op jit(solution)/shard_map/all_gather | solution.py:181
  199.6 428.4 %all-reduce.6.cloned.1.call-start = ((), (), s32[]{:S(2)}) async-start(), calls=%async_computation.19 | async-start | bytes 8388608 | tf_op jit(solution)/shard_map/psum | solution.py:205
  536.1 217.9 %reduce-scatter.9.cloned.1.call-start = ((), (), s32[]{:S(2)}) async-start(), calls=%async_computation.18 | async-start | bytes 2621440 | tf_op jit(solution)/shard_map/reduce_scatter | solution.py:187
  544.0 232.0 %all-reduce.8.cloned.1.call-start = ((), (), s32[]{:S(2)}) async-start(), calls=%async_computation.20 | async-start | bytes 4194304 | tf_op jit(solution)/shard_map/psum | solution.py:261
  717.3 140.0 %reduce-scatter.13.cloned.1.call-start = ((), (), s32[]{:S(2)}) async-start(), calls=%async_computation.22 | async-start | bytes 540672 | tf_op jit(solution)/shard_map/reduce_scatter | solution.py:269
  719.3 218.3 %reduce-scatter.15.cloned.1.call-start = ((), (), s32[]{:S(2)}) async-start(), calls=%async_computation.23 | async-start | bytes 540672 | tf_op jit(solution)/shard_map/reduce_scatter | solution.py:272
  721.2 298.4 %reduce-scatter.11.cloned.1.call-start = ((), (), s32[]{:S(2)}) async-start(), calls=%async_computation.21 | async-start | bytes 2162688 | tf_op jit(solution)/shard_map/reduce_scatter | solution.py:266
  724.1 377.5 %reduce-scatter.17.cloned.1.call-start = ((), (), s32[]{:S(2)}) async-start(), calls=%async_computation.24 | async-start | bytes 2162688 | tf_op jit(solution)/shard_map/reduce_scatter | solution.py:275
  729.5 461.0 %reduce-scatter.19.cloned.1.call-start = ((), (), s32[]{:S(2)}) async-start(), calls=%async_computation.25 | async-start | bytes 5947392 | tf_op jit(solution)/shard_map/reduce_scatter | solution.py:210
  737.7 541.0 %reduce-scatter.21.cloned.1.call-start = ((), (), s32[]{:S(2)}) async-start(), calls=%async_computation.26 | async-start | bytes 5947392 | tf_op jit(solution)/shard_map/reduce_scatter | solution.py:213
  745.9 621.7 %reduce-scatter.23.cloned.1.call-start = ((), (), s32[]{:S(2)}) async-start(), calls=%async_computation.27 | async-start | bytes 5947392 | tf_op jit(solution)/shard_map/reduce_scatter | solution.py:216
  758.3 24.8 %all-to-all-start.2 = ((bf16[32,16,512]{2,1,0:T(8,128)(2,1)}), bf16[32,16,512]{2,1,0:T(8,128)(2,1)S(1)}, u32[]{:S(2)}, u32[]{:S(2)}) async-start(bf16[32,16,512]{2,1,0:T(8,128)(2,1)} %bitcast.196), calls=%async_computation.3 | async-start | bytes 1048576 | tf_op jit(solution)/shard_map/all_to_all | solution.py:283
  780.5 161.0 %copy-start.20 = (bf16[2048]{0:T(1024)(128)(2,1)S(1)}, bf16[2048]{0:T(1024)(128)(2,1)}, u32[]{:S(2)}) copy-start(bf16[2048]{0:T(1024)(128)(2,1)} %get-tuple-element.247) | copy-start | bytes 12292
  783.1 223.4 %all-to-all-start.4 = ((bf16[32,16,512]{2,1,0:T(8,128)(2,1)}), bf16[32,16,512]{2,1,0:T(8,128)(2,1)S(1)}, u32[]{:S(2)}, u32[]{:S(2)}) async-start(bf16[32,16,512]{2,1,0:T(8,128)(2,1)} %bitcast.25), calls=%async_computation.5 | async-start | bytes 1048576 | tf_op jit(solution)/shard_map/all_to_all | solution.py:284
  938.9 430.3 %copy-start.1 = (bf16[512,512]{1,0:T(8,128)(2,1)S(1)}, bf16[512,512]{1,0:T(8,128)(2,1)}, u32[]{:S(2)}) copy-start(bf16[512,512]{1,0:T(8,128)(2,1)} %param.17) | copy-start | bytes 1572868
  (25 other events, 189.8 us)
Sparse Core Ops, SparseCore 0:
  50.7 28.4 all-gather.21
  81.5 44.0 all-gather.11
  127.9 43.2 all-gather.13
  176.3 153.2 all-gather.23
  331.7 49.4 all-gather.15
  383.3 47.4 all-gather.17
  433.0 29.7 all-gather.25
  465.0 48.4 all-gather.19
  536.2 91.7 all-reduce.5
  630.3 29.4 reduce-scatter.8
  717.5 58.4 all-reduce.7
  780.3 77.0 reduce-scatter.12
  861.2 76.3 reduce-scatter.14
  941.3 78.1 reduce-scatter.10
  1023.3 78.2 reduce-scatter.16
  1105.7 84.7 reduce-scatter.18
  1194.1 84.6 reduce-scatter.20
  1282.8 84.6 reduce-scatter.22
